TPU v7x, 256 devices: a whole 4x4x8 slice. The times are simulated.
256 devices in a mesh: layer: 2 (over z_lo), row: 8 (over y, core), col: 16 (over z_hi, x).
Axes of the slice: x: 4, y: 4, z: 8 (z_hi: 4, z_lo: 2; z = z_hi * 2 + z_lo), core: 2. Of those that a mesh axis runs over, the one named last changes fastest.
Arguments:
- matrix: float32 [16384, 16384], P('row', 'col'), may hold values from -1.5 to 1.5, as said below
Outputs:
- square_panel: float32 [16384, 512], P('row', 'layer')
- new_panel: float32 [16384, 512], P('row', 'layer')
Inputs may be any that keep to these rules, and one draw needn't show every extreme that they name: `matrix`: entries off the diagonal are of order 0.5 / sqrt(16384); the diagonal's magnitudes lie between 0.6 and 1 with either sign.
All inputs are finite; a program needn't handle non-finite values.
Results may differ from a plain program's by a relative error of at most 0.000076.
Values sent between devices are 32-bit elements; how exact they have to be, the bound alone decides.
A program may use at most 128 MiB of HBM per device.

v0:
```python
import jax
import jax.numpy as jnp
from jax import lax
from jax.sharding import PartitionSpec as P

PW = 512


def from_root(shard, axis, root):
    mine = lax.axis_index(axis) == root
    return lax.psum(jnp.where(mine, shard, jnp.zeros_like(shard)), axis)


def matmul_high(left_side, right_side):
    return jnp.dot(
        left_side, right_side, precision=lax.Precision.HIGHEST, preferred_element_type=jnp.float32
    )


def body(matrix):
    block_cols = matrix.shape[1]
    layers = lax.axis_size("layer")
    col_ratio = lax.axis_size("col") // lax.axis_size("row")
    col_index = lax.axis_index("col")
    layer_index = lax.axis_index("layer")
    half_width = PW // layers
    root_row = col_index // col_ratio
    offset = col_index % col_ratio * block_cols
    panel_full = from_root(matrix[:, :PW], "col", 0)
    own_cols = lax.dynamic_slice_in_dim(panel_full, layer_index * half_width, half_width, 1)
    depth_rows = block_cols // layers
    first_row = offset + layer_index * depth_rows
    panel_slab = from_root(
        lax.dynamic_slice_in_dim(panel_full, first_row, depth_rows, 0), "row", root_row
    )
    local_cols = lax.dynamic_slice_in_dim(matrix, layer_index * depth_rows, depth_rows, 1)
    square_full = lax.psum(matmul_high(local_cols, panel_slab), ("layer", "col"))
    square_slab = from_root(
        lax.dynamic_slice_in_dim(square_full, first_row, depth_rows, 0), "row", root_row
    )
    update = lax.psum_scatter(
        matmul_high(local_cols, square_slab), "layer", scatter_dimension=1, tiled=True
    )
    update = lax.psum(update, "col")
    square = lax.dynamic_slice_in_dim(square_full, layer_index * half_width, half_width, 1)
    new_panel = (3.0 * own_cols - update) * 0.5
    return (square, new_panel)


def solution(mesh):
    placed = (P("row", "col"),)
    return jax.shard_map(
        body,
        mesh=mesh,
        in_specs=placed,
        out_specs=(P("row", "layer"), P("row", "layer")),
        check_vma=False,
    )
```

profile of v0, /device:TPU:16, one launch (start us, length us, event | category | flops | bytes accessed | tf_op | source)
XLA Modules:
  0.0 809.4 jit_solution(460881230599396828)
XLA Ops:
  7.2 0.0 all-reduce.6.cloned.1.call-start
  7.2 4.6 slice_select_fusion
  11.9 0.0 all-reduce.6.cloned.1.call-update
  11.9 0.0 all-reduce.8.cloned.1.call-start
  12.0 224.7 %all-reduce.6.cloned.1.call-done = f32[2048,512]{1,0:T(8,128)} async-done(((f32[2048,512]{1,0:T(8,128)}), f32[2048,512]{1,0:T(8,128)}) %all-reduce.6.cloned.1.call-update) | async-done | bytes 4194320 | tf_op jit(solution)/shard_map/psum | solution.py:11
  236.6 2.3 dynamic-slice_select_fusion.1
  238.9 0.0 all-reduce.8.cloned.1.call-update
  239.0 0.0 all-reduce.10.cloned.1.call-start
  239.0 61.4 %all-reduce.8.cloned.1.call-done = f32[512,512]{1,0:T(8,128)} async-done(((f32[512,512]{1,0:T(8,128)}), f32[512,512]{1,0:T(8,128)}) %all-reduce.8.cloned.1.call-update) | async-done | bytes 1048592 | tf_op jit(solution)/shard_map/psum | solution.py:11
  300.4 10.1 %fusion.2 = f32[2048,512]{1,0:T(8,128)} fusion(f32[512,512]{1,0:T(8,128)} %all-reduce.8.cloned.1.call-done, f32[2048,1024]{1,0:T(8,128)} %param.1, s32[]{:T(128)S(6)} %select_n.42), kind=kOutput, calls=%fused_computation.3 | convolution fusion | flops 6442450944 | bytes 9437188 | tf_op jit(solution)/shard_map/dot_general | solution.py:15
  310.5 0.0 all-reduce.10.cloned.1.call-update
  310.5 0.0 all-reduce.12.cloned.1.call-start
  310.6 167.7 %all-reduce.10.cloned.1.call-done = f32[2048,512]{1,0:T(8,128)} async-done(((f32[2048,512]{1,0:T(8,128)}), f32[2048,512]{1,0:T(8,128)}) %all-reduce.10.cloned.1.call-update) | async-done | bytes 4194320 | tf_op jit(solution)/shard_map/psum | solution.py:37
  478.2 2.3 dynamic-slice_select_fusion
  480.5 0.0 all-reduce.12.cloned.1.call-update
  480.6 0.0 reduce-scatter.2.cloned.1.call-start
  480.6 61.5 %all-reduce.12.cloned.1.call-done = f32[512,512]{1,0:T(8,128)} async-done(((f32[512,512]{1,0:T(8,128)}), f32[512,512]{1,0:T(8,128)}) %all-reduce.12.cloned.1.call-update) | async-done | bytes 1048592 | tf_op jit(solution)/shard_map/psum | solution.py:11
  542.1 10.1 %fusion = f32[2048,512]{1,0:T(8,128)} fusion(f32[512,512]{1,0:T(8,128)} %all-reduce.12.cloned.1.call-done, f32[2048,1024]{1,0:T(8,128)} %param.1, s32[]{:T(128)S(6)} %select_n.42), kind=kOutput, calls=%fused_computation.1 | convolution fusion | flops 6442450944 | bytes 9437188 | tf_op jit(solution)/shard_map/dot_general | solution.py:15
  552.2 0.0 reduce-scatter.2.cloned.1.call-update
  552.2 0.0 all-reduce.14.cloned.1.call-start
  552.2 62.9 %reduce-scatter.2.cloned.1.call-done = f32[2048,256]{1,0:T(8,128)} async-done(((f32[2048,512]{1,0:T(8,128)}), f32[2048,256]{1,0:T(8,128)}) %reduce-scatter.2.cloned.1.call-update) | async-done | bytes 2097168 | tf_op jit(solution)/shard_map/reduce_scatter | solution.py:41
  615.2 3.0 constant_dynamic-slice_fusion
  618.3 180.5 %all-reduce.14.cloned.1.call-done = f32[2048,256]{1,0:T(8,128)} async-done(((f32[2048,256]{1,0:T(8,128)}), f32[2048,256]{1,0:T(8,128)}) %all-reduce.14.cloned.1.call-update) | async-done | bytes 2097168 | tf_op jit(solution)/shard_map/psum | solution.py:44
  798.7 3.8 subtract_multiply_fusion
  (1 shorter events, 0.0 us)
Async XLA Ops:
  7.2 229.5 %all-reduce.6.cloned.1.call-start = ((), (), s32[]{:S(2)}) async-start(), calls=%async_computation.1 | async-start | bytes 8388608 | tf_op jit(solution)/shard_map/psum | solution.py:11
  11.9 288.5 %all-reduce.8.cloned.1.call-start = ((), (), s32[]{:S(2)}) async-start(), calls=%async_computation.2 | async-start | bytes 2097152 | tf_op jit(solution)/shard_map/psum | solution.py:11
  239.0 239.3 %all-reduce.10.cloned.1.call-start = ((), (), s32[]{:S(2)}) async-start(), calls=%async_computation.3 | async-start | bytes 8388608 | tf_op jit(solution)/shard_map/psum | solution.py:37
  310.5 231.6 %all-reduce.12.cloned.1.call-start = ((), (), s32[]{:S(2)}) async-start(), calls=%async_computation.4 | async-start | bytes 2097152 | tf_op jit(solution)/shard_map/psum | solution.py:11
  480.6 134.6 %reduce-scatter.2.cloned.1.call-start = ((), (), s32[]{:S(2)}) async-start(), calls=%async_computation.5 | async-start | bytes 6291456 | tf_op jit(solution)/shard_map/reduce_scatter | solution.py:41
  552.2 246.5 %all-reduce.14.cloned.1.call-start = ((), (), s32[]{:S(2)}) async-start(), calls=%async_computation.6 | async-start | bytes 4194304 | tf_op jit(solution)/shard_map/psum | solution.py:44
Sparse Core Ops, SparseCore 0:
  12.0 224.5 all-reduce.5
  239.6 60.7 all-reduce.7
  310.6 167.5 all-reduce.9
  481.0 61.0 all-reduce.11
  552.3 62.8 reduce-scatter.1
  617.7 180.9 all-reduce.13
where the time goes:
time: 810 us; the launch traced here: 809 us
  waiting for transfers between devices  759 us (94%)
  matrix products  20.1 us (2%)
  between operations  14.2 us (2%)
  other arithmetic  13 us (2%)
    psum x3, waiting for transfers between devices, from_root(): return lax.psum(jnp.where(mine, shard, jnp.zeros_like(shard)), axis)  348 us
    psum x1, waiting for transfers between devices, body(): update = lax.psum(update, 'col')  180 us
    psum x1, waiting for transfers between devices, body(): lax.psum(matmul_high(local_cols, panel_slab), ('layer', 'col'))  168 us
    reduce_scatter x1, waiting for transfers between devices, body(): lax.psum_scatter(matmul_high(local_cols, square_slab), 'layer', scatter_d...  62.9 us
    dot_general x2, matrix products, matmul_high(): jnp.dot(left_side, right_side, precision=lax.Precision.HIGHEST, preferred...  20.1 us
  transfers between devices with their start and end apart: 6, of which 6 were waited for; matrix products, arithmetic and copies ran while one was open for 0% of the time, Pallas kernels for 0%

commit v1 on v0

--- a/solution.py
+++ b/solution.py
@@ -34,7 +34,9 @@
         lax.dynamic_slice_in_dim(panel_full, first_row, depth_rows, 0), "row", root_row
     )
     local_cols = lax.dynamic_slice_in_dim(matrix, layer_index * depth_rows, depth_rows, 1)
-    square_full = lax.psum(matmul_high(local_cols, panel_slab), ("layer", "col"))
+    square_full = matmul_high(local_cols, panel_slab)
+    for mesh_axis in ("col", "layer"):
+        square_full = lax.psum(square_full, mesh_axis)
     square_slab = from_root(
         lax.dynamic_slice_in_dim(square_full, first_row, depth_rows, 0), "row", root_row
     )

time: 810 us -> 988 us (1.22)
  waiting for transfers between devices: 759 us -> 937 us
    psum x1 -> x2, waiting for transfers between devices: 168 us -> 344 us  [body(): square_full = lax.psum(square_full, mesh_axis)]
  transfers between devices with their start and end apart: 6 -> 7, of which waited for: 6 -> 7; matrix products, arithmetic and copies ran while one was open for 0% -> 0% of each run, Pallas kernels for 0% -> 0%
where the time goes in v1:
time: 988 us
  waiting for transfers between devices  937 us (95%)
  matrix products  20.2 us (2%)
  between operations  14.2 us (1%)
  other arithmetic  13 us (1%)
    psum x3, waiting for transfers between devices, from_root(): return lax.psum(jnp.where(mine, shard, jnp.zeros_like(shard)), axis)  351 us
    psum x2, waiting for transfers between devices, body(): square_full = lax.psum(square_full, mesh_axis)  344 us
    psum x1, waiting for transfers between devices, body(): update = lax.psum(update, 'col')  179 us
    reduce_scatter x1, waiting for transfers between devices, body(): lax.psum_scatter(matmul_high(local_cols, square_slab), 'layer', scatter_d...  62.9 us
    dot_general x2, matrix products, matmul_high(): jnp.dot(left_side, right_side, precision=lax.Precision.HIGHEST, preferred...  20.2 us
  transfers between devices with their start and end apart: 7, of which 7 were waited for; matrix products, arithmetic and copies ran while one was open for 0% of the time, Pallas kernels for 0%

profile of v1, /device:TPU:16, one launch (start us, length us, event | category | flops | bytes accessed | tf_op | source)
XLA Modules:
  0.0 987.8 jit_solution(2636592461347693603)
XLA Ops:
  7.2 0.0 all-reduce.7.cloned.1.call-start
  7.2 4.6 slice_select_fusion
  11.9 0.0 all-reduce.7.cloned.1.call-update
  11.9 0.0 all-reduce.9.cloned.1.call-start
  12.0 224.7 %all-reduce.7.cloned.1.call-done = f32[2048,512]{1,0:T(8,128)} async-done(((f32[2048,512]{1,0:T(8,128)}), f32[2048,512]{1,0:T(8,128)}) %all-reduce.7.cloned.1.call-update) | async-done | bytes 4194320 | tf_op jit(solution)/shard_map/psum | solution.py:11
  236.6 2.3 dynamic-slice_select_fusion.1
  239.0 0.0 all-reduce.11.cloned.1.call-start
  239.0 61.4 %all-reduce.9.cloned.1.call-done = f32[512,512]{1,0:T(8,128)} async-done(((f32[512,512]{1,0:T(8,128)}), f32[512,512]{1,0:T(8,128)}) %all-reduce.9.cloned.1.call-update) | async-done | bytes 1048592 | tf_op jit(solution)/shard_map/psum | solution.py:11
  300.4 10.1 %fusion.2 = f32[2048,512]{1,0:T(8,128)} fusion(f32[512,512]{1,0:T(8,128)} %all-reduce.9.cloned.1.call-done, f32[2048,1024]{1,0:T(8,128)} %param.1, s32[]{:T(128)S(6)} %select_n.42), kind=kOutput, calls=%fused_computation.3 | convolution fusion | flops 6442450944 | bytes 9437188 | tf_op jit(solution)/shard_map/dot_general | solution.py:15
  310.5 0.0 all-reduce.11.cloned.1.call-update
  310.5 0.0 all-reduce.13.cloned.1.call-start
  310.6 225.2 %all-reduce.11.cloned.1.call-done = f32[2048,512]{1,0:T(8,128)} async-done(((f32[2048,512]{1,0:T(8,128)}), f32[2048,512]{1,0:T(8,128)}) %all-reduce.11.cloned.1.call-update) | async-done | bytes 4194320 | tf_op jit(solution)/shard_map/psum | solution.py:39
  535.8 0.0 all-reduce.13.cloned.1.call-update
  535.8 0.0 all-reduce.15.cloned.1.call-start
  535.9 118.7 %all-reduce.13.cloned.1.call-done = f32[2048,512]{1,0:T(8,128)} async-done(((f32[2048,512]{1,0:T(8,128)}), f32[2048,512]{1,0:T(8,128)}) %all-reduce.13.cloned.1.call-update) | async-done | bytes 4194320 | tf_op jit(solution)/shard_map/psum | solution.py:39
  654.5 2.3 dynamic-slice_select_fusion
  656.9 0.0 reduce-scatter.2.cloned.1.call-start
  656.9 64.7 %all-reduce.15.cloned.1.call-done = f32[512,512]{1,0:T(8,128)} async-done(((f32[512,512]{1,0:T(8,128)}), f32[512,512]{1,0:T(8,128)}) %all-reduce.15.cloned.1.call-update) | async-done | bytes 1048592 | tf_op jit(solution)/shard_map/psum | solution.py:11
  721.6 10.1 %fusion = f32[2048,512]{1,0:T(8,128)} fusion(f32[512,512]{1,0:T(8,128)} %all-reduce.15.cloned.1.call-done, f32[2048,1024]{1,0:T(8,128)} %param.1, s32[]{:T(128)S(6)} %select_n.42), kind=kOutput, calls=%fused_computation.1 | convolution fusion | flops 6442450944 | bytes 9437188 | tf_op jit(solution)/shard_map/dot_general | solution.py:15
  731.7 0.0 all-reduce.17.cloned.1.call-start
  731.7 62.9 %reduce-scatter.2.cloned.1.call-done = f32[2048,256]{1,0:T(8,128)} async-done(((f32[2048,512]{1,0:T(8,128)}), f32[2048,256]{1,0:T(8,128)}) %reduce-scatter.2.cloned.1.call-update) | async-done | bytes 2097168 | tf_op jit(solution)/shard_map/reduce_scatter | solution.py:43
  794.7 3.0 constant_dynamic-slice_fusion
  797.7 179.5 %all-reduce.17.cloned.1.call-done = f32[2048,256]{1,0:T(8,128)} async-done(((f32[2048,256]{1,0:T(8,128)}), f32[2048,256]{1,0:T(8,128)}) %all-reduce.17.cloned.1.call-update) | async-done | bytes 2097168 | tf_op jit(solution)/shard_map/psum | solution.py:46
  977.2 3.8 subtract_multiply_fusion
  (4 shorter events, 0.1 us)
Async XLA Ops:
  7.2 229.5 %all-reduce.7.cloned.1.call-start = ((), (), s32[]{:S(2)}) async-start(), calls=%async_computation.1 | async-start | bytes 8388608 | tf_op jit(solution)/shard_map/psum | solution.py:11
  11.9 288.5 %all-reduce.9.cloned.1.call-start = ((), (), s32[]{:S(2)}) async-start(), calls=%async_computation.2 | async-start | bytes 2097152 | tf_op jit(solution)/shard_map/psum | solution.py:11
  239.0 296.9 %all-reduce.11.cloned.1.call-start = ((), (), s32[]{:S(2)}) async-start(), calls=%async_computation.3 | async-start | bytes 8388608 | tf_op jit(solution)/shard_map/psum | solution.py:39
  310.5 344.0 %all-reduce.13.cloned.1.call-start = ((), (), s32[]{:S(2)}) async-start(), calls=%async_computation.4 | async-start | bytes 8388608 | tf_op jit(solution)/shard_map/psum | solution.py:39
  535.8 185.7 %all-reduce.15.cloned.1.call-start = ((), (), s32[]{:S(2)}) async-start(), calls=%async_computation.5 | async-start | bytes 2097152 | tf_op jit(solution)/shard_map/psum | solution.py:11
  656.9 137.8 %reduce-scatter.2.cloned.1.call-start = ((), (), s32[]{:S(2)}) async-start(), calls=%async_computation.6 | async-start | bytes 6291456 | tf_op jit(solution)/shard_map/reduce_scatter | solution.py:43
  731.7 245.5 %all-reduce.17.cloned.1.call-start = ((), (), s32[]{:S(2)}) async-start(), calls=%async_computation.7 | async-start | bytes 4194304 | tf_op jit(solution)/shard_map/psum | solution.py:46
Sparse Core Ops, SparseCore 0:
  12.0 224.5 all-reduce.6
  239.6 60.7 all-reduce.8
  310.7 225.0 all-reduce.10
  538.4 116.0 all-reduce.12
  657.3 64.2 all-reduce.14
  731.8 62.8 reduce-scatter.1
  797.3 179.8 all-reduce.16
